TPU v7x, 32 devices: a whole 2x2x4 slice. The times are simulated.
32 devices in a mesh: grp: 2 (over x), row: 16 (over z, y, core).
Axes of the slice: x: 2, y: 2, z: 4, core: 2. Of those that a mesh axis runs over, the one named last changes fastest.
Arguments:
- excitations: bfloat16 [32, 8192, 128], P('grp', 'row'), parts along dimension 0, may hold values from -0.005859375 to 0.005859375
- valence_orb: bfloat16 [2048, 128], P(('grp', 'row')), parts along dimension 0, may hold values from -6 to 6
- conduction_orb: bfloat16 [2048, 8192], P(('grp', 'row')), parts along dimension 0, may hold values from -6 to 6
- screened: bfloat16 [2048, 1024], P(('grp', 'row')), parts along dimension 0, may hold values from -0.005859375 to 0.005859375
Outputs:
- action: bfloat16 [32, 8192, 128], P('grp', 'row'), parts along dimension 0
There are 2 independent parts, one for each index of `grp`. A program takes and returns all parts, laid end to end along the dimension named above; each array names one. Nothing has to cross between parts.
All inputs are finite; a program needn't handle non-finite values.
Results may differ from a plain program's by a relative error of at most 0.0064.
Values may be sent and summed in bfloat16 or wider, within the bound.
A program may use at most 64 MiB of HBM per device.

v0:
```python
import math
import jax
import jax.numpy as jnp
from jax import lax
from jax.sharding import PartitionSpec as P


def over_blocks(total_rows, step_fn, initial):
    span_size = math.gcd(total_rows, 2048)
    block_count = total_rows // span_size
    if block_count == 1:
        return step_fn(initial, 0, span_size)
    return lax.fori_loop(
        0, block_count, lambda index, carry: step_fn(carry, index * span_size, span_size), initial
    )


def density_rows(flat_exc, batch, valence_rows, cond_rows):
    total_rows = valence_rows.shape[0]
    cond_local = cond_rows.shape[1]
    initial = jnp.zeros((batch, total_rows), jnp.float32)

    def step_fn(carry, offset, span_size):
        val_block = lax.dynamic_slice_in_dim(valence_rows, offset, span_size, 0)
        cond_block = lax.dynamic_slice_in_dim(cond_rows, offset, span_size, 0)
        mixed = lax.dot_general(
            flat_exc, val_block, (((1,), (1,)), ((), ())), preferred_element_type=jnp.float32
        )
        mixed = mixed.reshape(batch, cond_local, span_size)
        summed = jnp.sum(mixed * cond_block.T.astype(jnp.float32)[None], axis=1)
        return lax.dynamic_update_slice_in_dim(carry, summed, offset, 1)

    return over_blocks(total_rows, step_fn, initial)


def projection(carry, valence_rows, cond_rows, field_cols):
    total_rows = valence_rows.shape[0]
    batch = field_cols.shape[0]
    cond_local = cond_rows.shape[1]

    def step_fn(inner, offset, span_size):
        val_block = lax.dynamic_slice_in_dim(valence_rows, offset, span_size, 0)
        cond_block = lax.dynamic_slice_in_dim(cond_rows, offset, span_size, 0)
        field_block = lax.dynamic_slice_in_dim(field_cols, offset, span_size, 1)
        pair = (
            cond_block.T.astype(jnp.float32)[None] * field_block.astype(jnp.float32)[:, None, :]
        ).astype(jnp.bfloat16)
        pair = pair.reshape(batch * cond_local, span_size)
        return inner + jnp.dot(pair, val_block, preferred_element_type=jnp.float32)

    return over_blocks(total_rows, step_fn, carry)


def body(excitations, valence_orb, conduction_orb, screened):
    batch, cond_local, valence = excitations.shape
    flat_exc = excitations.reshape(batch * cond_local, valence)
    valence_whole = lax.all_gather(valence_orb, "row", axis=0, tiled=True)
    cond_rows = lax.all_to_all(conduction_orb, "row", split_axis=1, concat_axis=0, tiled=True)
    partial_density = density_rows(flat_exc, batch, valence_whole, cond_rows)
    density_whole = lax.psum(partial_density, "row").astype(jnp.bfloat16)
    field_mine = lax.dot_general(
        density_whole, screened, (((1,), (1,)), ((), ())), preferred_element_type=jnp.float32
    ).astype(jnp.bfloat16)
    initial = jnp.zeros((batch * cond_local, valence), jnp.float32)
    summed = projection(
        initial, valence_whole, cond_rows, lax.all_gather(field_mine, "row", axis=1, tiled=True)
    )
    return summed.reshape(batch, cond_local, valence).astype(jnp.bfloat16)


def solution(mesh):
    in_specs = (
        P("grp", "row", None),
        P(("grp", "row"), None),
        P(("grp", "row"), None),
        P(("grp", "row"), None),
    )
    out_specs = P("grp", "row", None)
    return jax.shard_map(body, mesh=mesh, in_specs=in_specs, out_specs=out_specs, check_vma=False)
```

profile of v0, /device:TPU:0, one launch (start us, length us, event | category | flops | bytes accessed | tf_op | source)
XLA Modules:
  0.0 141.2 jit_solution(12085013585132656083)
XLA Ops:
  0.0 0.0 copy-start
  0.0 0.0 copy-start.2
  0.0 2.5 %copy.15 = bf16[8,16,8,512]{3,2,0,1:T(8,128)(2,1)} copy(bf16[8,16,8,512]{3,2,1,0:T(8,128)(2,1)} %bitcast.26) | data formatting | bytes 2097152 | tf_op jit(solution)/shard_map/all_to_all | solution.py:58
  2.5 7.4 %all-to-all-start = ((bf16[64,16,512]{2,0,1:T(8,128)(2,1)}), bf16[64,16,512]{2,0,1:T(8,128)(2,1)S(1)}, u32[]{:S(2)}, u32[]{:S(2)}) async-start(bf16[64,16,512]{2,0,1:T(8,128)(2,1)} %bitcast.25), calls=%async_computation | async-start | bytes 2097152 | tf_op jit(solution)/shard_map/all_to_all | solution.py:58
  9.9 0.0 copy-done.2
  9.9 34.5 %all_gather.6 = bf16[1024,128]{1,0:T(8,128)(2,1)S(1)} all-gather(bf16[64,128]{1,0:T(8,128)(2,1)S(1)} %copy-done.2), channel_id=1, replica_groups=mesh['grp'=2,'row'=16] {'row'}, dimensions={0}, use_global_device_ids=true | all-gather | bytes 278528 | tf_op jit(solution)/shard_map/all_gather | solution.py:57
  44.4 0.0 all-to-all-done
  44.4 1.6 %convert_element_type.41 = f32[64,16,512]{2,0,1:T(8,128)} convert(bf16[64,16,512]{2,0,1:T(8,128)(2,1)S(1)} %all-to-all-done) | non-fusion elementwise | flops 524288 | bytes 3145728 | tf_op jit(solution)/shard_map/convert_element_type | solution.py:46
  46.0 2.9 %copy.11 = f32[512,1024]{1,0:T(8,128)} copy(f32[512,1024]{0,1:T(8,128)} %bitcast.24) | data formatting | bytes 4194304 | tf_op jit(solution)/shard_map/convert_element_type | solution.py:46
  48.9 0.0 copy-done
  48.9 0.0 copy-start.1
  48.9 6.0 %multiply_reduce_fusion = f32[16,1024]{1,0:T(8,128)S(1)} fusion(f32[512,1024]{1,0:T(8,128)} %copy.11, bf16[16,512,128]{2,1,0:T(8,128)(2,1)S(1)} %copy-done, bf16[1024,128]{1,0:T(8,128)(2,1)S(1)} %all_gather.6), kind=kOutput, calls=%fused_computation.1 | convolution fusion | flops 2164244480 | bytes 4521984 | tf_op jit(solution)/shard_map/dot_general | solution.py:26
  54.9 61.8 %psum.7 = bf16[16,1024]{1,0:T(8,128)(2,1)S(1)} all-reduce(f32[16,1024]{1,0:T(8,128)S(1)} %multiply_reduce_fusion), channel_id=1, replica_groups=mesh['grp'=2,'row'=16] {'row'}, use_global_device_ids=true, to_apply=%region_1.0 | all-reduce | flops 16384 | bytes 98304 | tf_op jit(solution)/shard_map/psum | solution.py:60
  116.7 0.0 copy-done.1
  116.7 0.1 fusion.4
  116.9 17.3 %all-gather = bf16[16,64,16]{1,2,0:T(8,128)(2,1)S(1)} all-gather(bf16[1,64,16]{1,2,0:T(8,128)(2,1)S(1)} %fusion.4), channel_id=1, replica_groups=mesh['grp'=2,'row'=16] {'row'}, dimensions={0}, use_global_device_ids=true | all-gather | bytes 34816 | tf_op jit(solution)/shard_map/all_gather | solution.py:66
  134.2 0.1 reshape.19
  134.3 6.9 %fusion.3 = bf16[16,512,128]{2,1,0:T(8,128)(2,1)} fusion(f32[16,1024]{1,0:T(8,128)S(1)} %bitcast.27, f32[512,1024]{1,0:T(8,128)} %copy.11, bf16[1024,128]{1,0:T(8,128)(2,1)S(1)} %all_gather.6), kind=kOutput, calls=%fused_computation.5 | convolution fusion | flops 2165309440 | bytes 4521984 | tf_op jit(solution)/shard_map/dot_general | solution.py:49
  (1 shorter events, 0.0 us)
Async XLA Ops:
  0.0 48.9 %copy-start = (bf16[16,512,128]{2,1,0:T(8,128)(2,1)S(1)}, bf16[16,512,128]{2,1,0:T(8,128)(2,1)}, u32[]{:S(2)}) copy-start(bf16[16,512,128]{2,1,0:T(8,128)(2,1)} %param.4) | copy-start | bytes 6291460
  0.0 9.9 %copy-start.2 = (bf16[64,128]{1,0:T(8,128)(2,1)S(1)}, bf16[64,128]{1,0:T(8,128)(2,1)}, u32[]{:S(2)}) copy-start(bf16[64,128]{1,0:T(8,128)(2,1)} %param.5) | copy-start | bytes 49156
  2.5 41.9 %all-to-all-start = ((bf16[64,16,512]{2,0,1:T(8,128)(2,1)}), bf16[64,16,512]{2,0,1:T(8,128)(2,1)S(1)}, u32[]{:S(2)}, u32[]{:S(2)}) async-start(bf16[64,16,512]{2,0,1:T(8,128)(2,1)} %bitcast.25), calls=%async_computation | async-start | bytes 2097152 | tf_op jit(solution)/shard_map/all_to_all | solution.py:58
  48.9 67.8 %copy-start.1 = (bf16[64,1024]{1,0:T(8,128)(2,1)S(1)}, bf16[64,1024]{1,0:T(8,128)(2,1)}, u32[]{:S(2)}) copy-start(bf16[64,1024]{1,0:T(8,128)(2,1)} %param.7) | copy-start | bytes 393220
where the time goes:
time: 142 us; the launch traced here: 141 us
  blocking collectives  114 us (80%)
  matrix products  13.1 us (9%)
  starting transfers between devices  7.41 us (5%)
  local copies, waits for them, and re-layouts  5.54 us (4%)
  other arithmetic  1.6 us (1%)
    psum x1, blocking collectives, body(): density_whole = lax.psum(partial_density, 'row').astype(jnp.bfloat16)  61.8 us
    all_gather x1, blocking collectives, body(): valence_whole = lax.all_gather(valence_orb, 'row', axis=0, tiled=True)  34.5 us
    all_gather x1, blocking collectives, body(): lax.all_gather(field_mine, 'row', axis=1, tiled=True)  17.3 us
    all_to_all x1, starting transfers between devices, body(): lax.all_to_all(conduction_orb, 'row', split_axis=1, concat_axis=0, tiled=...  7.41 us
    dot_general x1, matrix products, step_fn(): return inner + jnp.dot(pair, val_block, preferred_element_type=jnp.float32)  6.93 us
    dot_general x1, matrix products, step_fn(): lax.dot_general(flat_exc, val_block, (((1,), (1,)), ((), ())), preferred_...  6.01 us
    convert_element_type x1, local copies, waits for them, and re-layouts, step_fn(): cond_block.T.astype(jnp.float32)[None]  2.94 us
  transfers between devices with their start and end apart: 1, of which 0 were waited for; matrix products, arithmetic and copies ran while one was open for 0% of the time, Pallas kernels for 0%

commit v1 on v0

--- a/solution.py
+++ b/solution.py
@@ -55,7 +55,12 @@
     batch, cond_local, valence = excitations.shape
     flat_exc = excitations.reshape(batch * cond_local, valence)
     valence_whole = lax.all_gather(valence_orb, "row", axis=0, tiled=True)
-    cond_rows = lax.all_to_all(conduction_orb, "row", split_axis=1, concat_axis=0, tiled=True)
+    cond_rows = jnp.concatenate(
+        lax.all_to_all(
+            jnp.stack(jnp.split(conduction_orb, lax.axis_size("row"), axis=1)), "row", 0, 0
+        ),
+        axis=0,
+    )
     partial_density = density_rows(flat_exc, batch, valence_whole, cond_rows)
     density_whole = lax.psum(partial_density, "row").astype(jnp.bfloat16)
     field_mine = lax.dot_general(

time: 142 us -> 164 us (1.15)
  local copies, waits for them, and re-layouts: 5.54 us -> 26.8 us
    unnamed x6 -> x21, local copies, waits for them, and re-layouts: 0.01 us -> 22.3 us
    all_to_all x1 -> x0, local copies, waits for them, and re-layouts: 2.47 us -> none  [body(): lax.all_to_all(conduction_orb, 'row', split_axis=1, concat_axis=0, tiled=...]
where the time goes in v1:
time: 164 us; the launch traced here: 163 us
  blocking collectives  114 us (70%)
  local copies, waits for them, and re-layouts  26.8 us (16%)
  matrix products  13.1 us (8%)
  starting transfers between devices  7.41 us (5%)
  other arithmetic  1.68 us (1%)
    psum x1, blocking collectives, body(): density_whole = lax.psum(partial_density, 'row').astype(jnp.bfloat16)  61.8 us
    all_gather x1, blocking collectives, body(): valence_whole = lax.all_gather(valence_orb, 'row', axis=0, tiled=True)  34.5 us
    unnamed x21, local copies, waits for them, and re-layouts  22.3 us
    all_gather x1, blocking collectives, body(): lax.all_gather(field_mine, 'row', axis=1, tiled=True)  17.3 us
    all_to_all x1, starting transfers between devices, body(): lax.all_to_all(jnp.stack(jnp.split(conduction_orb, lax.axis_size('row'),...  7.41 us
    dot_general x1, matrix products, step_fn(): return inner + jnp.dot(pair, val_block, preferred_element_type=jnp.float32)  6.93 us
    dot_general x1, matrix products, step_fn(): lax.dot_general(flat_exc, val_block, (((1,), (1,)), ((), ())), preferred_...  6.01 us
  transfers between devices with their start and end apart: 1, of which 0 were waited for; matrix products, arithmetic and copies ran while one was open for 0% of the time, Pallas kernels for 0%

profile of v1, /device:TPU:0, one launch (start us, length us, event | category | flops | bytes accessed | tf_op | source)
XLA Modules:
  0.0 162.6 jit_solution(14286315960880834663)
XLA Ops:
  0.0 0.0 copy-start
  0.0 0.0 copy-start.2
  0.0 1.6 %bitcast_dynamic-update-slice_fusion.15 = bf16[16,64,512]{2,1,0:T(8,128)(2,1)} fusion(bf16[64,8192]{1,0:T(8,128)(2,1)} %param.6), kind=kLoop, calls=%fused_computation.26 | loop fusion | bytes 131072
  1.6 1.5 bitcast_dynamic-update-slice_fusion.14
  3.1 1.5 bitcast_dynamic-update-slice_fusion.13
  4.6 1.5 bitcast_dynamic-update-slice_fusion.12
  6.1 1.5 bitcast_dynamic-update-slice_fusion.11
  7.5 1.5 bitcast_dynamic-update-slice_fusion.10
  9.0 1.5 bitcast_dynamic-update-slice_fusion.9
  10.5 1.5 bitcast_dynamic-update-slice_fusion.8
  11.9 1.5 bitcast_dynamic-update-slice_fusion.7
  13.4 1.5 bitcast_dynamic-update-slice_fusion.6
  14.9 1.5 bitcast_dynamic-update-slice_fusion.5
  16.4 1.5 bitcast_dynamic-update-slice_fusion.4
  17.8 1.5 bitcast_dynamic-update-slice_fusion.3
  19.3 1.5 bitcast_dynamic-update-slice_fusion.2
  20.8 1.5 bitcast_dynamic-update-slice_fusion.1
  22.3 1.5 bitcast_dynamic-update-slice_fusion
  23.7 7.4 %all-to-all-start = ((bf16[16,64,512]{2,1,0:T(8,128)(2,1)}), bf16[16,64,512]{2,1,0:T(8,128)(2,1)S(1)}, u32[]{:S(2)}, u32[]{:S(2)}) async-start(bf16[16,64,512]{2,1,0:T(8,128)(2,1)} %bitcast_dynamic-update-slice_fusion), calls=%async_computation | async-start | bytes 2097152 | tf_op jit(solution)/shard_map/all_to_all | solution.py:59
  31.2 0.0 copy-done.2
  31.2 34.5 %all_gather.6 = bf16[1024,128]{1,0:T(8,128)(2,1)S(1)} all-gather(bf16[64,128]{1,0:T(8,128)(2,1)S(1)} %copy-done.2), channel_id=1, replica_groups=mesh['grp'=2,'row'=16] {'row'}, dimensions={0}, use_global_device_ids=true | all-gather | bytes 278528 | tf_op jit(solution)/shard_map/all_gather | solution.py:57
  65.6 0.0 all-to-all-done
  65.6 1.7 %bitcast_convert_fusion = f32[1024,512]{1,0:T(8,128)} fusion(bf16[16,64,512]{2,1,0:T(8,128)(2,1)S(1)} %all-to-all-done), kind=kLoop, calls=%fused_computation.8 | loop fusion | flops 524288 | bytes 3145728 | tf_op jit(solution)/shard_map/convert_element_type | solution.py:46
  67.3 2.9 %copy.8 = f32[1024,512]{0,1:T(8,128)} copy(f32[1024,512]{1,0:T(8,128)} %bitcast_convert_fusion) | data formatting | bytes 4194304 | tf_op jit(solution)/shard_map/convert_element_type | solution.py:46
  70.2 0.0 copy-done
  70.2 0.0 copy-start.1
  70.2 6.0 %multiply_reduce_fusion = f32[16,1024]{1,0:T(8,128)S(1)} fusion(f32[512,1024]{1,0:T(8,128)} %bitcast.51, bf16[16,512,128]{2,1,0:T(8,128)(2,1)S(1)} %copy-done, bf16[1024,128]{1,0:T(8,128)(2,1)S(1)} %all_gather.6), kind=kOutput, calls=%fused_computation.1 | convolution fusion | flops 2164244480 | bytes 4521984 | tf_op jit(solution)/shard_map/dot_general | solution.py:26
  76.3 61.8 %psum.7 = bf16[16,1024]{1,0:T(8,128)(2,1)S(1)} all-reduce(f32[16,1024]{1,0:T(8,128)S(1)} %multiply_reduce_fusion), channel_id=1, replica_groups=mesh['grp'=2,'row'=16] {'row'}, use_global_device_ids=true, to_apply=%region_1.0 | all-reduce | flops 16384 | bytes 98304 | tf_op jit(solution)/shard_map/psum | solution.py:65
  138.1 0.0 copy-done.1
  138.1 0.1 fusion.4
  138.2 17.3 %all-gather = bf16[16,64,16]{1,2,0:T(8,128)(2,1)S(1)} all-gather(bf16[1,64,16]{1,2,0:T(8,128)(2,1)S(1)} %fusion.4), channel_id=1, replica_groups=mesh['grp'=2,'row'=16] {'row'}, dimensions={0}, use_global_device_ids=true | all-gather | bytes 34816 | tf_op jit(solution)/shard_map/all_gather | solution.py:71
  155.5 0.1 reshape.17
  155.6 6.9 %fusion.3 = bf16[16,512,128]{2,1,0:T(8,128)(2,1)} fusion(f32[16,1024]{1,0:T(8,128)S(1)} %bitcast.53, f32[512,1024]{1,0:T(8,128)} %bitcast.52, bf16[1024,128]{1,0:T(8,128)(2,1)S(1)} %all_gather.6), kind=kOutput, calls=%fused_computation.5 | convolution fusion | flops 2165309440 | bytes 4521984 | tf_op jit(solution)/shard_map/dot_general | solution.py:49
  (1 shorter events, 0.0 us)
Async XLA Ops:
  0.0 70.2 %copy-start = (bf16[16,512,128]{2,1,0:T(8,128)(2,1)S(1)}, bf16[16,512,128]{2,1,0:T(8,128)(2,1)}, u32[]{:S(2)}) copy-start(bf16[16,512,128]{2,1,0:T(8,128)(2,1)} %param.4) | copy-start | bytes 6291460
  0.0 31.2 %copy-start.2 = (bf16[64,128]{1,0:T(8,128)(2,1)S(1)}, bf16[64,128]{1,0:T(8,128)(2,1)}, u32[]{:S(2)}) copy-start(bf16[64,128]{1,0:T(8,128)(2,1)} %param.5) | copy-start | bytes 49156
  23.7 41.9 %all-to-all-start = ((bf16[16,64,512]{2,1,0:T(8,128)(2,1)}), bf16[16,64,512]{2,1,0:T(8,128)(2,1)S(1)}, u32[]{:S(2)}, u32[]{:S(2)}) async-start(bf16[16,64,512]{2,1,0:T(8,128)(2,1)} %bitcast_dynamic-update-slice_fusion), calls=%async_computation | async-start | bytes 2097152 | tf_op jit(solution)/shard_map/all_to_all | solution.py:59
  70.2 67.8 %copy-start.1 = (bf16[64,1024]{1,0:T(8,128)(2,1)S(1)}, bf16[64,1024]{1,0:T(8,128)(2,1)}, u32[]{:S(2)}) copy-start(bf16[64,1024]{1,0:T(8,128)(2,1)} %param.7) | copy-start | bytes 393220
